TPU v7x, 128 devices: a whole 4x4x4 slice. The times are simulated.
128 devices in a mesh: grp: 8 (over y, x_lo), bal: 16 (over x_hi, z, core).
Axes of the slice: x: 4 (x_hi: 2, x_lo: 2; x = x_hi * 2 + x_lo), y: 4, z: 4, core: 2. Of those that a mesh axis runs over, the one named last changes fastest.
Arguments:
- events: bfloat16 [8, 8192, 512], P('grp', 'bal'), may hold values from -6 to 6
- cotangent: bfloat16 [8, 8192, 512], P('grp', 'bal'), may hold values from -6 to 6
- lengths: int32 [8, 16], P('grp'), may hold values from 1 to 16, as said below
- gain_in: float32 [512], replicated, may hold values from 0.1 to 1.9
- w_proj: bfloat16 [512, 2048], replicated, may hold values from -0.25 to 0.25
- gain_attn: float32 [512], replicated, may hold values from 0.1 to 1.9
- w_out: bfloat16 [512, 512], replicated, may hold values from -0.25 to 0.25
Outputs:
- d_x: bfloat16 [8, 8192, 512], P('grp', 'bal')
- grad_proj: float32 [512, 2048], replicated
- grad_out: float32 [512, 512], replicated
- grad_gain_in: float32 [512], replicated
- grad_gain_attn: float32 [512], replicated
Inputs may be any that keep to these rules, and one draw needn't show every extreme that they name: A group's 16 lengths count blocks of 64 events and sum to 128; in every group one length equals 16.
All inputs are finite; a program needn't handle non-finite values.
Results may differ from a plain program's by a relative error of at most 0.013.
Values may be sent and summed in bfloat16 or wider, within the bound.
No kernel may reach another device: no remote copies, remote signals or barrier semaphores. Data moves between devices by JAX's collectives and lax.ppermute only.
A program may use at most 256 MiB of HBM per device.

v0:
```python
import math
import jax
import jax.numpy as jnp
from jax import lax
from jax.sharding import PartitionSpec as P

HEADS = 8
BLOCK = 64
LEN_BLK = 16
epsilon = 1e-06


def norm_rows(values):
    mean_value = jnp.mean(values, axis=-1, keepdims=True)
    centred = values - mean_value
    rstd = lax.rsqrt(jnp.mean(centred * centred, axis=-1, keepdims=True) + epsilon)
    return (centred * rstd, rstd)


def silu_slope(values):
    sigma = jax.nn.sigmoid(values)
    return sigma * (1.0 + values * (1.0 - sigma))


def norm_back(grad, normed, rstd):
    return rstd * (
        grad
        - jnp.mean(grad, axis=-1, keepdims=True)
        - normed * jnp.mean(grad * normed, axis=-1, keepdims=True)
    )


def contract_rows(left, right):
    return lax.dot_general(
        left, right, (((0,), (0,)), ((), ())), preferred_element_type=jnp.float32
    )


def contract_cols(left, right):
    return lax.dot_general(
        left, right, (((1,), (1,)), ((), ())), preferred_element_type=jnp.float32
    )


def project_rows(rows, gain_in, w_proj):
    normed, rstd_in = norm_rows(rows.astype(jnp.float32))
    scaled = (normed * gain_in).astype(jnp.bfloat16)
    hidden = jnp.dot(scaled, w_proj, preferred_element_type=jnp.float32)
    active = jax.nn.silu(hidden).astype(jnp.bfloat16)
    return (normed, rstd_in, scaled, hidden, active)


def output_rows(attn, upper, grads_out, gain_attn, w_out):
    normed, rstd = norm_rows(attn.astype(jnp.float32))
    upper_wide = upper.astype(jnp.float32)
    mixed = (normed * gain_attn * upper_wide).astype(jnp.bfloat16)
    d_mixed = contract_cols(grads_out, w_out)
    d_upper = d_mixed * normed * gain_attn
    d_attn = norm_back(d_mixed * gain_attn * upper_wide, normed, rstd).astype(jnp.bfloat16)
    out_term = contract_rows(mixed, grads_out)
    gain_term = jnp.sum(d_mixed * normed * upper_wide, axis=0)
    return (d_upper, d_attn, out_term, gain_term)


def input_rows(grads_out, d_act, hidden, normed, rstd_in, scaled, gain_in, w_proj):
    d_hidden = (d_act * silu_slope(hidden)).astype(jnp.bfloat16)
    proj_term = contract_rows(scaled, d_hidden)
    d_scaled = contract_cols(d_hidden, w_proj)
    d_rows = (
        grads_out.astype(jnp.float32) + norm_back(d_scaled * gain_in, normed, rstd_in)
    ).astype(jnp.bfloat16)
    gain_term = jnp.sum(d_scaled * normed, axis=0)
    return (d_rows, proj_term, gain_term)


def attend_forward(query, keys, values, allowed):
    head_width = query.shape[1] // HEADS
    scale = head_width ** (-0.5)
    outputs = []
    for head in range(HEADS):
        columns = slice(head * head_width, (head + 1) * head_width)
        scores = contract_cols(query[:, columns], keys[:, columns]) * scale
        weights = (jax.nn.silu(scores) * allowed).astype(jnp.bfloat16)
        outputs.append(jnp.dot(weights, values[:, columns], preferred_element_type=jnp.float32))
    return jnp.concatenate(outputs, axis=1).astype(jnp.bfloat16)


def attend_backward(query, keys, values, grad_attn, allowed):
    head_width = query.shape[1] // HEADS
    scale = head_width ** (-0.5)
    grads_query, grads_keys, grads_values = ([], [], [])
    for head in range(HEADS):
        columns = slice(head * head_width, (head + 1) * head_width)
        query_head = query[:, columns]
        key_head = keys[:, columns]
        grad_head = grad_attn[:, columns]
        scores = contract_cols(query_head, key_head) * scale
        weights = (jax.nn.silu(scores) * allowed).astype(jnp.bfloat16)
        grad_weights = contract_cols(grad_head, values[:, columns])
        grad_scores = (grad_weights * silu_slope(scores) * allowed).astype(jnp.bfloat16)
        grads_values.append(contract_rows(weights, grad_head).astype(jnp.bfloat16))
        grads_query.append(
            (jnp.dot(grad_scores, key_head, preferred_element_type=jnp.float32) * scale).astype(
                jnp.bfloat16
            )
        )
        grads_keys.append((contract_rows(grad_scores, query_head) * scale).astype(jnp.bfloat16))
    return (
        jnp.concatenate(grads_query, axis=1),
        jnp.concatenate(grads_keys, axis=1),
        jnp.concatenate(grads_values, axis=1),
    )


def lookup(table, positions):
    entries = jnp.arange(table.shape[0], dtype=jnp.int32)
    picked = jnp.where(entries[None, :] == positions[:, None], table[None, :], 0)
    return jnp.sum(picked, axis=1)


def regroup(table, rows):
    blocks = rows.reshape(table.shape[1], -1)
    moved = jnp.dot(table, blocks, preferred_element_type=jnp.float32)
    return moved.astype(jnp.bfloat16).reshape(-1, rows.shape[1])


def pack_histories(seq_lengths):

    def advance(state, length_now):
        device_rank, held_blocks = state
        fresh = held_blocks + length_now > LEN_BLK
        device_rank = device_rank + fresh.astype(jnp.int32)
        held_blocks = jnp.where(fresh, 0, held_blocks) + length_now
        return ((device_rank, held_blocks), device_rank)

    start_state = (jnp.int32(0), jnp.int32(0))
    final_state, ranks = lax.scan(advance, start_state, seq_lengths)
    return ranks


def held_tiles_map(tile_fn, live_tiles, inputs, tile_rows):
    count = inputs[0].shape[0] // tile_rows
    pieces = tuple((array.reshape((count, tile_rows) + array.shape[1:]) for array in inputs))

    def blank_fn(parts):
        return jax.tree.map(jnp.zeros_like, tile_fn(parts))

    def each_tile(item):
        position, parts = item
        return lax.cond(position < live_tiles, tile_fn, blank_fn, parts)

    return lax.map(each_tile, (jnp.arange(count, dtype=jnp.int32), pieces))


def flatten_tiles(array):
    return array.reshape((-1,) + array.shape[2:])


def whole_layer(rows, grads_out, allowed, live_tiles, tile_rows, gain_in, w_proj, gain_attn, w_out):
    width = rows.shape[1]
    first = held_tiles_map(
        lambda parts: project_rows(parts[0], gain_in, w_proj), live_tiles, (rows,), tile_rows
    )
    normed, rstd_in, scaled, hidden, active = jax.tree.map(flatten_tiles, first)
    upper = active[:, :width]
    values = active[:, width : 2 * width]
    query = active[:, 2 * width : 3 * width]
    keys = active[:, 3 * width :]
    attn = attend_forward(query, keys, values, allowed)
    second = held_tiles_map(
        lambda parts: output_rows(parts[0], parts[1], parts[2], gain_attn, w_out),
        live_tiles,
        (attn, upper, grads_out),
        tile_rows,
    )
    d_upper = flatten_tiles(second[0])
    d_attn = flatten_tiles(second[1])
    out_term = jnp.sum(second[2], axis=0)
    gain_attn_term = jnp.sum(second[3], axis=0)
    d_query, d_keys, d_values = attend_backward(query, keys, values, d_attn, allowed)
    d_act = jnp.concatenate(
        [
            d_upper,
            d_values.astype(jnp.float32),
            d_query.astype(jnp.float32),
            d_keys.astype(jnp.float32),
        ],
        axis=1,
    )
    third = held_tiles_map(
        lambda parts: input_rows(
            parts[0], parts[1], parts[2], parts[3], parts[4], parts[5], gain_in, w_proj
        ),
        live_tiles,
        (grads_out, d_act, hidden, normed, rstd_in, scaled),
        tile_rows,
    )
    d_rows = flatten_tiles(third[0])
    proj_term = jnp.sum(third[1], axis=0)
    gain_in_term = jnp.sum(third[2], axis=0)
    return (d_rows, (proj_term, out_term, gain_in_term, gain_attn_term))


def per_device(events, cotangent, lengths, gain_in, w_proj, gain_attn, w_out):
    peers = lax.axis_size("bal")
    own_index = lax.axis_index("bal")
    local_rows = events[0]
    local_grads = cotangent[0]
    local_blocks = local_rows.shape[0] // BLOCK
    slots = LEN_BLK // peers
    seq_lengths = lengths[0]
    targets = pack_histories(seq_lengths)
    ends = jnp.cumsum(seq_lengths)
    device_ids = jnp.arange(peers, dtype=jnp.int32)
    range_starts = jnp.sum(
        jnp.where(targets[None, :] < device_ids[:, None], seq_lengths[None, :], 0), axis=1
    )
    range_sizes = jnp.sum(
        jnp.where(targets[None, :] == device_ids[:, None], seq_lengths[None, :], 0), axis=1
    )
    flat_blocks = own_index + peers * jnp.arange(local_blocks, dtype=jnp.int32)
    owner_seq = jnp.sum((ends[None, :] <= flat_blocks[:, None]).astype(jnp.int32), axis=1)
    owner = lookup(targets, owner_seq)
    slot_index = (flat_blocks - lookup(range_starts, owner)) // peers
    slot_ids = jnp.arange(peers * slots, dtype=jnp.int32)
    send_table = (slot_ids[:, None] == (owner * slots + slot_index)[None, :]).astype(jnp.bfloat16)
    mine_start = lookup(range_starts, own_index[None])[0]
    mine_size = lookup(range_sizes, own_index[None])[0]
    block_order = jnp.arange(LEN_BLK, dtype=jnp.int32)
    from_slot = (mine_start + block_order) % peers * slots + block_order // peers
    take_table = (from_slot[:, None] == slot_ids[None, :]).astype(jnp.bfloat16)
    return_table = jnp.transpose(take_table)
    home_table = jnp.transpose(send_table)
    block_seq = jnp.sum(
        (ends[None, :] <= (mine_start + block_order)[:, None]).astype(jnp.int32), axis=1
    )
    block_seq = jnp.where(block_order < mine_size, block_seq, -1)
    row_seq = jnp.repeat(block_seq, BLOCK)
    positions = jnp.arange(LEN_BLK * BLOCK, dtype=jnp.int32)
    allowed = (
        (row_seq[:, None] == row_seq[None, :])
        & (row_seq[:, None] >= 0)
        & (positions[None, :] <= positions[:, None])
    ).astype(jnp.float32)
    tile_blocks = math.gcd(LEN_BLK, max(1, 256 // BLOCK))
    live_tiles = (mine_size + tile_blocks - 1) // tile_blocks
    got_rows, got_grads = (
        lax.all_to_all(
            regroup(send_table, local_rows), "bal", split_axis=0, concat_axis=0, tiled=True
        ),
        lax.all_to_all(
            regroup(send_table, local_grads), "bal", split_axis=0, concat_axis=0, tiled=True
        ),
    )
    held_rows = regroup(take_table, got_rows)
    held_grads = regroup(take_table, got_grads)
    d_held, terms = whole_layer(
        held_rows,
        held_grads,
        allowed,
        live_tiles,
        tile_blocks * BLOCK,
        gain_in,
        w_proj,
        gain_attn,
        w_out,
    )
    came_back = lax.all_to_all(
        regroup(return_table, d_held), "bal", split_axis=0, concat_axis=0, tiled=True
    )
    d_rows = regroup(home_table, came_back)
    sums = lax.psum((terms[0], terms[1], terms[2], terms[3]), ("grp", "bal"))
    divisor = float(lax.axis_size("grp") * peers)
    return (
        d_rows[None],
        sums[0] / divisor,
        sums[1] / divisor,
        sums[2] / divisor,
        sums[3] / divisor,
    )


def solution(mesh):
    placed = (P("grp", "bal", None), P("grp", "bal", None), P("grp", None), P(), P(), P(), P())
    return jax.shard_map(
        per_device,
        mesh=mesh,
        in_specs=placed,
        out_specs=(P("grp", "bal", None), P(), P(), P(), P()),
        check_vma=False,
    )
```

profile of v0, /device:TPU:1, one launch (start us, length us, event | category | flops | bytes accessed | tf_op | source)
XLA Modules:
  0.0 636.9 jit_solution(15162623421532527161)
XLA Ops:
  7.2 42.6 %while.66 = (s32[]{:T(128)}, s32[]{:T(128)}, s32[]{:T(128)}, s32[16]{0:T(128)S(1)}, s32[16]{0:T(128)}) while((s32[]{:T(128)}, s32[]{:T(128)}, s32[]{:T(128)}, s32[16]{0:T(128)S(1)}, s32[16]{0:T(128)}) %tuple.198), condition=%wide.region_3.4_spmd.clone, body=%wide.region_2.3_spmd.sunk.clone | while | flops 8 | bytes 148 | solution.py:137
  55.1 9.3 %all-to-all-start.1 = ((bf16[16,64,512]{2,1,0:T(8,128)(2,1)}), bf16[16,64,512]{2,1,0:T(8,128)(2,1)S(1)}, u32[]{:S(2)}, u32[]{:S(2)}) async-start(bf16[16,64,512]{2,1,0:T(8,128)(2,1)} %bitcast.70), calls=%async_computation.1 | async-start | bytes 2097152 | tf_op jit(solution)/shard_map/all_to_all | solution.py:248
  70.0 11.6 %all-to-all-done.1 = bf16[16,64,512]{2,1,0:T(8,128)(2,1)S(1)} async-done(((bf16[16,64,512]{2,1,0:T(8,128)(2,1)}), bf16[16,64,512]{2,1,0:T(8,128)(2,1)S(1)}, u32[]{:S(2)}, u32[]{:S(2)}) %all-to-all-start.1) | async-done | bytes 1048608 | tf_op jit(solution)/shard_map/all_to_all | solution.py:248
  91.9 70.2 %while.67 = (s32[]{:T(128)}, f32[4,256,512]{2,1,0:T(8,128)}, f32[4,256,1]{1,2,0:T(1,128)}, bf16[4,256,512]{2,1,0:T(8,128)(2,1)}, f32[4,256,2048]{2,1,0:T(8,128)}...) while((s32[]{:T(128)}, f32[4,256,512]{2,1,0:T(8,128)}, ...), condition=%wide.region_16.17_spmd.clone, body=%wide.region_11.16_spmd.sunk.clone | while | flops 541589760 | bytes 17060060 | solution.py:152
  93.2 9.2 %conditional.9 = (f32[1,256,512]{2,1,0:T(8,128)S(1)}, f32[1,256,1]{1,2,0:T(1,128)}, bf16[1,256,512]{2,1,0:T(8,128)(2,1)S(1)}, f32[1,256,2048]{2,1,0:T(8,128)}, bf16[1,256,2048]{2,1,0:T(8,128)(2,1)S(1)}) conditional(s32[]{:T(128)} %convert_element_type.475, () %tuple.157, (bf16[4,256,512]{2,1,0:T(8,128)(2,1)}, s32[]{:T(128)}, f32[512]{0:T(512)S(1)}, ...), branch_computations={%region_12.12_spmd, %region_13.15_spmd} | conditional | flops 541589760 | bytes 9190964 | solution.py:150
  110.8 9.2 %conditional.9 = (f32[1,256,512]{2,1,0:T(8,128)S(1)}, f32[1,256,1]{1,2,0:T(1,128)}, bf16[1,256,512]{2,1,0:T(8,128)(2,1)S(1)}, f32[1,256,2048]{2,1,0:T(8,128)}, bf16[1,256,2048]{2,1,0:T(8,128)(2,1)S(1)}) conditional(s32[]{:T(128)} %convert_element_type.475, () %tuple.157, (bf16[4,256,512]{2,1,0:T(8,128)(2,1)}, s32[]{:T(128)}, f32[512]{0:T(512)S(1)}, ...), branch_computations={%region_12.12_spmd, %region_13.15_spmd} | conditional | flops 541589760 | bytes 9190964 | solution.py:150
  128.4 9.2 %conditional.9 = (f32[1,256,512]{2,1,0:T(8,128)S(1)}, f32[1,256,1]{1,2,0:T(1,128)}, bf16[1,256,512]{2,1,0:T(8,128)(2,1)S(1)}, f32[1,256,2048]{2,1,0:T(8,128)}, bf16[1,256,2048]{2,1,0:T(8,128)(2,1)S(1)}) conditional(s32[]{:T(128)} %convert_element_type.475, () %tuple.157, (bf16[4,256,512]{2,1,0:T(8,128)(2,1)}, s32[]{:T(128)}, f32[512]{0:T(512)S(1)}, ...), branch_computations={%region_12.12_spmd, %region_13.15_spmd} | conditional | flops 541589760 | bytes 9190964 | solution.py:150
  145.9 9.2 %conditional.9 = (f32[1,256,512]{2,1,0:T(8,128)S(1)}, f32[1,256,1]{1,2,0:T(1,128)}, bf16[1,256,512]{2,1,0:T(8,128)(2,1)S(1)}, f32[1,256,2048]{2,1,0:T(8,128)}, bf16[1,256,2048]{2,1,0:T(8,128)(2,1)S(1)}) conditional(s32[]{:T(128)} %convert_element_type.475, () %tuple.157, (bf16[4,256,512]{2,1,0:T(8,128)(2,1)}, s32[]{:T(128)}, f32[512]{0:T(512)S(1)}, ...), branch_computations={%region_12.12_spmd, %region_13.15_spmd} | conditional | flops 541589760 | bytes 9190964 | solution.py:150
  186.4 19.1 %select_convert_fusion.8 = (bf16[1024,1024]{1,0:T(8,128)(2,1)S(1)}, bf16[1024,1024]{1,0:T(8,128)(2,1)}, bf16[1024,1024]{1,0:T(8,128)(2,1)}, bf16[1024,1024]{1,0:...) fusion(pred[1024]{0:T(1024)(128)(4,1)S(1)} %broadcast_compare_f, ...), kind=kOutput, calls=%fused_computation.122 | convolution fusion | flops 197132288 | bytes 50865152 | tf_op jit(solution)/shard_map/dot_general | solution.py:40
  237.3 35.1 %while.68 = (s32[]{:T(128)}, f32[4,256,512]{2,1,0:T(8,128)}, bf16[4,256,512]{2,1,0:T(8,128)(2,1)}, f32[4,512,512]{2,1,0:T(8,128)}, f32[4,512]{1,0:T(4,128)S(1)},...) while((s32[]{:T(128)}, f32[4,256,512]{2,1,0:T(8,128)}, ...), condition=%wide.region_25.26_spmd.clone, body=%wide.region_17.25_spmd.sunk.clone | while | flops 273415936 | bytes 9736943 | solution.py:152
  372.0 5.6 pad_maximum_fusion
  377.8 67.9 %while.69 = (s32[]{:T(128)}, bf16[4,256,512]{2,1,0:T(8,128)(2,1)S(1)}, f32[4,512,2048]{2,1,0:T(8,128)}, f32[4,512]{1,0:T(4,128)S(1)}, s32[4]{0:T(128)S(1)}, /*in...) while((s32[]{:T(128)}, ...), condition=%wide.region_32.33_spmd.clone, body=%wide.region_26.32_spmd.sunk.clone | while | flops 1085013504 | bytes 26500880 | solution.py:152
  379.3 10.9 %conditional.11 = (bf16[1,256,512]{2,1,0:T(8,128)(2,1)S(1)}, f32[1,512,2048]{2,1,0:T(8,128)}, f32[1,512]{1,0:T(1,128)S(1)}) conditional(s32[]{:T(128)} %convert_element_type.477, () %tuple.167, (bf16[4,256,512]{2,1,0:T(8,128)(2,1)}, s32[]{:T(128)}, f32[4,256,1]{1,2,0:T(1,128)}, f32[4,256,2048]{2,1,0:T(8,128)}, f32[4,256,2048]{2,1,0:T(8,128)}, ...), branch_computations={%region_27.27_spmd, %region_28.31_spmd} | conditional | flops 1085013504 | bytes 17583136 | solution.py:150
  384.7 5.5 convolution_bitcast_fusion.1
  396.1 10.9 %conditional.11 = (bf16[1,256,512]{2,1,0:T(8,128)(2,1)S(1)}, f32[1,512,2048]{2,1,0:T(8,128)}, f32[1,512]{1,0:T(1,128)S(1)}) conditional(s32[]{:T(128)} %convert_element_type.477, () %tuple.167, (bf16[4,256,512]{2,1,0:T(8,128)(2,1)}, s32[]{:T(128)}, f32[4,256,1]{1,2,0:T(1,128)}, f32[4,256,2048]{2,1,0:T(8,128)}, f32[4,256,2048]{2,1,0:T(8,128)}, ...), branch_computations={%region_27.27_spmd, %region_28.31_spmd} | conditional | flops 1085013504 | bytes 17583136 | solution.py:150
  401.6 5.5 convolution_bitcast_fusion.1
  413.1 11.0 %conditional.11 = (bf16[1,256,512]{2,1,0:T(8,128)(2,1)S(1)}, f32[1,512,2048]{2,1,0:T(8,128)}, f32[1,512]{1,0:T(1,128)S(1)}) conditional(s32[]{:T(128)} %convert_element_type.477, () %tuple.167, (bf16[4,256,512]{2,1,0:T(8,128)(2,1)}, s32[]{:T(128)}, f32[4,256,1]{1,2,0:T(1,128)}, f32[4,256,2048]{2,1,0:T(8,128)}, f32[4,256,2048]{2,1,0:T(8,128)}, ...), branch_computations={%region_27.27_spmd, %region_28.31_spmd} | conditional | flops 1085013504 | bytes 17583136 | solution.py:150
  418.5 5.5 convolution_bitcast_fusion.1
  430.0 11.0 %conditional.11 = (bf16[1,256,512]{2,1,0:T(8,128)(2,1)S(1)}, f32[1,512,2048]{2,1,0:T(8,128)}, f32[1,512]{1,0:T(1,128)S(1)}) conditional(s32[]{:T(128)} %convert_element_type.477, () %tuple.167, (bf16[4,256,512]{2,1,0:T(8,128)(2,1)}, s32[]{:T(128)}, f32[4,256,1]{1,2,0:T(1,128)}, f32[4,256,2048]{2,1,0:T(8,128)}, f32[4,256,2048]{2,1,0:T(8,128)}, ...), branch_computations={%region_27.27_spmd, %region_28.31_spmd} | conditional | flops 1085013504 | bytes 17583136 | solution.py:150
  435.5 5.5 convolution_bitcast_fusion.1
  445.7 10.1 %reduce_sum.224 = f32[512,2048]{1,0:T(8,128)} reduce(f32[4,512,2048]{2,1,0:T(8,128)} %get-tuple-element.445, f32[]{:T(128)} %constant.270.clone.1), dimensions={0}, to_apply=%region_33.34 | reduce | flops 3145728 | bytes 20971524 | tf_op jit(solution)/shard_map/reduce_sum | solution.py:199
  462.0 5.8 all-to-all-start.2
  467.8 73.7 %all-reduce = (f32[512]{0:T(512)S(1)}, f32[512]{0:T(512)S(1)}) all-reduce(f32[512]{0:T(512)S(1)} %reduce_sum.226, f32[512]{0:T(512)S(1)} %reduce_sum.227), channel_id=1, replica_groups=mesh['grp'=8,'bal'=16] {'grp','bal'}, use_global_device_ids=true, to_apply=%region_38.39 | all-reduce | flops 1024 | bytes 8192 | tf_op jit(solution)/shard_map/psum | solution.py:272
  544.6 79.3 %all-reduce.4.cloned.1.call-done = (f32[512,2048]{1,0:T(8,128)}, f32[512,512]{1,0:T(8,128)}) async-done(((f32[512,2048]{1,0:T(8,128)}, f32[512,512]{1,0:T(8,128)}), (f32[512,2048]{1,0:T(8,128)}, f32[512,512]{1,0:T(8,128)})) %all-reduce.4.cloned.1.call-update) | async-done | bytes 5242896 | tf_op jit(solution)/shard_map/psum | solution.py:272
  (412 shorter events, 374.3 us)
Async XLA Ops:
  7.2 60.8 %copy-start.36 = (bf16[1,512,512]{2,1,0:T(8,128)(2,1)S(1)}, bf16[1,512,512]{2,1,0:T(8,128)(2,1)}, u32[]{:S(2)}) copy-start(bf16[1,512,512]{2,1,0:T(8,128)(2,1)} %param.22) | copy-start | bytes 1572868
  52.0 16.6 %copy-start.40 = (s32[8]{0:T(128)}, s32[8]{0:T(128)S(1)}, u32[]{:S(2)}) copy-start(s32[8]{0:T(128)S(1)} %fusion.169) | copy-start | bytes 100
  55.1 26.5 %all-to-all-start.1 = ((bf16[16,64,512]{2,1,0:T(8,128)(2,1)}), bf16[16,64,512]{2,1,0:T(8,128)(2,1)S(1)}, u32[]{:S(2)}, u32[]{:S(2)}) async-start(bf16[16,64,512]{2,1,0:T(8,128)(2,1)} %bitcast.70), calls=%async_computation.1 | async-start | bytes 2097152 | tf_op jit(solution)/shard_map/all_to_all | solution.py:248
  67.0 163.3 %copy-start.42 = (s32[16]{0:T(128)}, s32[16]{0:T(128)S(1)}, u32[]{:S(2)}) copy-start(s32[16]{0:T(128)S(1)} %get-tuple-element.578) | copy-start | bytes 196
  81.6 147.0 %all-to-all-start = ((bf16[16,64,512]{2,1,0:T(8,128)(2,1)}), bf16[16,64,512]{2,1,0:T(8,128)(2,1)}, u32[]{:S(2)}, u32[]{:S(2)}) async-start(bf16[16,64,512]{2,1,0:T(8,128)(2,1)} %bitcast.66), calls=%async_computation | async-start | bytes 2097152 | tf_op jit(solution)/shard_map/all_to_all | solution.py:251
  86.6 537.4 %all-reduce.4.cloned.1.call-start = ((), (), s32[]{:S(2)}) async-start(), calls=%async_computation.3 | async-start | bytes 10485760 | tf_op jit(solution)/shard_map/psum | solution.py:272
  186.4 19.1 %copy-start.15 = (f32[1024,1024]{1,0:T(8,128)}, f32[1024,1024]{1,0:T(8,128)S(1)}, u32[]{:S(2)}) copy-start(f32[1024,1024]{1,0:T(8,128)S(1)} %fusion.155) | copy-start | bytes 12582916
  205.5 7.7 %copy-start.8 = (bf16[1024,1024]{1,0:T(8,128)(2,1)}, bf16[1024,1024]{1,0:T(8,128)(2,1)S(1)}, u32[]{:S(2)}) copy-start(bf16[1024,1024]{1,0:T(8,128)(2,1)S(1)} %get-tuple-element.573) | copy-start | bytes 6291460
  205.5 7.7 %copy-start.10 = (bf16[1024,1024]{1,0:T(8,128)(2,1)}, bf16[1024,1024]{1,0:T(8,128)(2,1)S(1)}, u32[]{:S(2)}) copy-start(bf16[1024,1024]{1,0:T(8,128)(2,1)S(1)} %get-tuple-element.574) | copy-start | bytes 6291460
  205.5 7.7 %copy-start.6 = (bf16[1024,1024]{1,0:T(8,128)(2,1)}, bf16[1024,1024]{1,0:T(8,128)(2,1)S(1)}, u32[]{:S(2)}) copy-start(bf16[1024,1024]{1,0:T(8,128)(2,1)S(1)} %get-tuple-element.572) | copy-start | bytes 6291460
  205.5 9.4 %copy-start.12 = (bf16[1024,1024]{1,0:T(8,128)(2,1)}, bf16[1024,1024]{1,0:T(8,128)(2,1)S(1)}, u32[]{:S(2)}) copy-start(bf16[1024,1024]{1,0:T(8,128)(2,1)S(1)} %get-tuple-element.575) | copy-start | bytes 6291460
  205.5 9.4 %copy-start.13 = (bf16[1024,1024]{1,0:T(8,128)(2,1)}, bf16[1024,1024]{1,0:T(8,128)(2,1)S(1)}, u32[]{:S(2)}) copy-start(bf16[1024,1024]{1,0:T(8,128)(2,1)S(1)} %get-tuple-element.569) | copy-start | bytes 6291460
  205.5 20.4 %copy-start.2 = (bf16[1024,1024]{1,0:T(8,128)(2,1)}, bf16[1024,1024]{1,0:T(8,128)(2,1)S(1)}, u32[]{:S(2)}) copy-start(bf16[1024,1024]{1,0:T(8,128)(2,1)S(1)} %get-tuple-element.576) | copy-start | bytes 6291460
  230.8 6.4 %copy-start.37 = (f32[512]{0:T(512)S(1)}, f32[512]{0:T(512)}, u32[]{:S(2)}) copy-start(f32[512]{0:T(512)} %param.26) | copy-start | bytes 6148
  272.4 5.3 copy-start.38
  282.7 5.2 copy-start.21
  359.1 5.1 copy-start.33
  359.1 5.2 copy-start.34
  359.1 5.4 copy-start.35
  372.0 5.8 copy-start.1
  372.0 5.8 copy-start.31
  459.6 8.2 %copy-start.39 = (f32[4,512]{1,0:T(4,128)S(1)}, f32[4,512]{1,0:T(4,128)}, u32[]{:S(2)}) copy-start(f32[4,512]{1,0:T(4,128)} %copy-done.38) | copy-start | bytes 24580
  460.2 83.1 %copy-start.41 = (s32[8]{0:T(128)S(1)}, s32[8]{0:T(128)}, u32[]{:S(2)}) copy-start(s32[8]{0:T(128)} %copy-done.40) | copy-start | bytes 100
  462.0 80.6 %all-to-all-start.2 = ((bf16[16,64,512]{2,1,0:T(8,128)(2,1)}), bf16[16,64,512]{2,1,0:T(8,128)(2,1)S(1)}, u32[]{:S(2)}, u32[]{:S(2)}) async-start(bf16[16,64,512]{2,1,0:T(8,128)(2,1)} %bitcast.74), calls=%async_computation.2 | async-start | bytes 2097152 | tf_op jit(solution)/shard_map/all_to_all | solution.py:268
  (25 other events, 87.1 us)
Sparse Core Ops, SparseCore 0:
  459.7 164.1 all-reduce.3
where the time goes:
time: 644 us; the launch traced here: 637 us
  matrix products  205 us (32%)
  local copies, waits for them, and re-layouts  132 us (20%)
  waiting for transfers between devices  90.9 us (14%)
  blocking collectives  73.7 us (11%)
  other arithmetic  70.4 us (11%)
  loops' own time  29.7 us (5%)
  starting transfers between devices  20.1 us (3%)
  between operations  16 us (2%)
    dot_general x24, matrix products, contract_cols(): lax.dot_general(left, right, (((1,), (1,)), ((), ())), preferred_element_...  103 us
    psum x1, waiting for transfers between devices, per_device(): sums = lax.psum((terms[0], terms[1], terms[2], terms[3]), ('grp', 'bal'))  79.3 us
    psum x1, blocking collectives, per_device(): sums = lax.psum((terms[0], terms[1], terms[2], terms[3]), ('grp', 'bal'))  73.7 us
    dynamic_update_slice x48, local copies, waits for them, and re-layouts, held_tiles_map(): return lax.map(each_tile, (jnp.arange(count, dtype=jnp.int32), pieces))  57.7 us
    dot_general x24, matrix products, contract_rows(): lax.dot_general(left, right, (((0,), (0,)), ((), ())), preferred_element_...  51.2 us
    another operation x1, loops' own time, pack_histories(): final_state, ranks = lax.scan(advance, start_state, seq_lengths)  20.9 us
    dynamic_slice x16, local copies, waits for them, and re-layouts, pack_histories(): final_state, ranks = lax.scan(advance, start_state, seq_lengths)  19.9 us
    dot_general x8, matrix products, attend_backward(): jnp.dot(grad_scores, key_head, preferred_element_type=jnp.float32) * scale  19.2 us
  transfers between devices with their start and end apart: 4, of which 2 were waited for; matrix products, arithmetic and copies ran while one was open for 23% of the time, Pallas kernels for 0%

commit v1 on v0

--- a/solution.py
+++ b/solution.py
@@ -269,7 +269,9 @@
         regroup(return_table, d_held), "bal", split_axis=0, concat_axis=0, tiled=True
     )
     d_rows = regroup(home_table, came_back)
-    sums = lax.psum((terms[0], terms[1], terms[2], terms[3]), ("grp", "bal"))
+    sums = (terms[0], terms[1], terms[2], terms[3])
+    for no in ("bal", "grp"):
+        sums = lax.psum(sums, axis_name=no)
     divisor = float(lax.axis_size("grp") * peers)
     return (
         d_rows[None],

time: 644 us -> 869 us (1.35)
  waiting for transfers between devices: 90.9 us -> 317 us
    psum x1 -> x2, waiting for transfers between devices: 79.3 us -> 306 us  [per_device(): sums = lax.psum(sums, axis_name=no)]
    psum x1 -> x2, blocking collectives: 73.7 us -> 70.1 us  [per_device(): sums = lax.psum(sums, axis_name=no)]
  transfers between devices with their start and end apart: 4 -> 5, of which waited for: 2 -> 3; matrix products, arithmetic and copies ran while one was open for 23% -> 17% of each run, Pallas kernels for 0% -> 0%
where the time goes in v1:
time: 869 us; the launch traced here: 862 us
  waiting for transfers between devices  317 us (36%)
  matrix products  205 us (24%)
  local copies, waits for them, and re-layouts  132 us (15%)
  other arithmetic  70.4 us (8%)
  blocking collectives  70.1 us (8%)
  loops' own time  29.7 us (3%)
  starting transfers between devices  22 us (3%)
  between operations  16.1 us (2%)
    psum x2, waiting for transfers between devices, per_device(): sums = lax.psum(sums, axis_name=no)  306 us
    dot_general x24, matrix products, contract_cols(): lax.dot_general(left, right, (((1,), (1,)), ((), ())), preferred_element_...  103 us
    psum x2, blocking collectives, per_device(): sums = lax.psum(sums, axis_name=no)  70.1 us
    dynamic_update_slice x48, local copies, waits for them, and re-layouts, held_tiles_map(): return lax.map(each_tile, (jnp.arange(count, dtype=jnp.int32), pieces))  57.7 us
    dot_general x24, matrix products, contract_rows(): lax.dot_general(left, right, (((0,), (0,)), ((), ())), preferred_element_...  51.2 us
    another operation x1, loops' own time, pack_histories(): final_state, ranks = lax.scan(advance, start_state, seq_lengths)  20.9 us
    dynamic_slice x16, local copies, waits for them, and re-layouts, pack_histories(): final_state, ranks = lax.scan(advance, start_state, seq_lengths)  19.9 us
    dot_general x8, matrix products, attend_backward(): jnp.dot(grad_scores, key_head, preferred_element_type=jnp.float32) * scale  19.2 us
  transfers between devices with their start and end apart: 5, of which 3 were waited for; matrix products, arithmetic and copies ran while one was open for 17% of the time, Pallas kernels for 0%

profile of v1, /device:TPU:1, one launch (start us, length us, event | category | flops | bytes accessed | tf_op | source)
XLA Modules:
  0.0 861.8 jit_solution(5402769518485513113)
XLA Ops:
  7.2 42.6 %while.66 = (s32[]{:T(128)}, s32[]{:T(128)}, s32[]{:T(128)}, s32[16]{0:T(128)S(1)}, s32[16]{0:T(128)}) while((s32[]{:T(128)}, s32[]{:T(128)}, s32[]{:T(128)}, s32[16]{0:T(128)S(1)}, s32[16]{0:T(128)}) %tuple.201), condition=%wide.region_3.4_spmd.clone, body=%wide.region_2.3_spmd.sunk.clone | while | flops 8 | bytes 148 | solution.py:137
  55.1 9.3 %all-to-all-start.1 = ((bf16[16,64,512]{2,1,0:T(8,128)(2,1)}), bf16[16,64,512]{2,1,0:T(8,128)(2,1)S(1)}, u32[]{:S(2)}, u32[]{:S(2)}) async-start(bf16[16,64,512]{2,1,0:T(8,128)(2,1)} %bitcast.70), calls=%async_computation.1 | async-start | bytes 2097152 | tf_op jit(solution)/shard_map/all_to_all | solution.py:248
  70.0 11.6 %all-to-all-done.1 = bf16[16,64,512]{2,1,0:T(8,128)(2,1)S(1)} async-done(((bf16[16,64,512]{2,1,0:T(8,128)(2,1)}), bf16[16,64,512]{2,1,0:T(8,128)(2,1)S(1)}, u32[]{:S(2)}, u32[]{:S(2)}) %all-to-all-start.1) | async-done | bytes 1048608 | tf_op jit(solution)/shard_map/all_to_all | solution.py:248
  91.9 70.2 %while.67 = (s32[]{:T(128)}, f32[4,256,512]{2,1,0:T(8,128)}, f32[4,256,1]{1,2,0:T(1,128)}, bf16[4,256,512]{2,1,0:T(8,128)(2,1)}, f32[4,256,2048]{2,1,0:T(8,128)}...) while((s32[]{:T(128)}, f32[4,256,512]{2,1,0:T(8,128)}, ...), condition=%wide.region_16.17_spmd.clone, body=%wide.region_11.16_spmd.sunk.clone | while | flops 541589760 | bytes 17060060 | solution.py:152
  93.2 9.2 %conditional.9 = (f32[1,256,512]{2,1,0:T(8,128)S(1)}, f32[1,256,1]{1,2,0:T(1,128)}, bf16[1,256,512]{2,1,0:T(8,128)(2,1)S(1)}, f32[1,256,2048]{2,1,0:T(8,128)}, bf16[1,256,2048]{2,1,0:T(8,128)(2,1)S(1)}) conditional(s32[]{:T(128)} %convert_element_type.475, () %tuple.157, (bf16[4,256,512]{2,1,0:T(8,128)(2,1)}, s32[]{:T(128)}, f32[512]{0:T(512)S(1)}, ...), branch_computations={%region_12.12_spmd, %region_13.15_spmd} | conditional | flops 541589760 | bytes 9190964 | solution.py:150
  110.8 9.2 %conditional.9 = (f32[1,256,512]{2,1,0:T(8,128)S(1)}, f32[1,256,1]{1,2,0:T(1,128)}, bf16[1,256,512]{2,1,0:T(8,128)(2,1)S(1)}, f32[1,256,2048]{2,1,0:T(8,128)}, bf16[1,256,2048]{2,1,0:T(8,128)(2,1)S(1)}) conditional(s32[]{:T(128)} %convert_element_type.475, () %tuple.157, (bf16[4,256,512]{2,1,0:T(8,128)(2,1)}, s32[]{:T(128)}, f32[512]{0:T(512)S(1)}, ...), branch_computations={%region_12.12_spmd, %region_13.15_spmd} | conditional | flops 541589760 | bytes 9190964 | solution.py:150
  128.4 9.2 %conditional.9 = (f32[1,256,512]{2,1,0:T(8,128)S(1)}, f32[1,256,1]{1,2,0:T(1,128)}, bf16[1,256,512]{2,1,0:T(8,128)(2,1)S(1)}, f32[1,256,2048]{2,1,0:T(8,128)}, bf16[1,256,2048]{2,1,0:T(8,128)(2,1)S(1)}) conditional(s32[]{:T(128)} %convert_element_type.475, () %tuple.157, (bf16[4,256,512]{2,1,0:T(8,128)(2,1)}, s32[]{:T(128)}, f32[512]{0:T(512)S(1)}, ...), branch_computations={%region_12.12_spmd, %region_13.15_spmd} | conditional | flops 541589760 | bytes 9190964 | solution.py:150
  145.9 9.2 %conditional.9 = (f32[1,256,512]{2,1,0:T(8,128)S(1)}, f32[1,256,1]{1,2,0:T(1,128)}, bf16[1,256,512]{2,1,0:T(8,128)(2,1)S(1)}, f32[1,256,2048]{2,1,0:T(8,128)}, bf16[1,256,2048]{2,1,0:T(8,128)(2,1)S(1)}) conditional(s32[]{:T(128)} %convert_element_type.475, () %tuple.157, (bf16[4,256,512]{2,1,0:T(8,128)(2,1)}, s32[]{:T(128)}, f32[512]{0:T(512)S(1)}, ...), branch_computations={%region_12.12_spmd, %region_13.15_spmd} | conditional | flops 541589760 | bytes 9190964 | solution.py:150
  186.4 19.1 %select_convert_fusion.8 = (bf16[1024,1024]{1,0:T(8,128)(2,1)S(1)}, bf16[1024,1024]{1,0:T(8,128)(2,1)}, bf16[1024,1024]{1,0:T(8,128)(2,1)}, bf16[1024,1024]{1,0:...) fusion(pred[1024]{0:T(1024)(128)(4,1)S(1)} %broadcast_compare_f, ...), kind=kOutput, calls=%fused_computation.122 | convolution fusion | flops 197132288 | bytes 50865152 | tf_op jit(solution)/shard_map/dot_general | solution.py:40
  237.3 35.1 %while.68 = (s32[]{:T(128)}, f32[4,256,512]{2,1,0:T(8,128)}, bf16[4,256,512]{2,1,0:T(8,128)(2,1)}, f32[4,512,512]{2,1,0:T(8,128)}, f32[4,512]{1,0:T(4,128)S(1)},...) while((s32[]{:T(128)}, f32[4,256,512]{2,1,0:T(8,128)}, ...), condition=%wide.region_25.26_spmd.clone, body=%wide.region_17.25_spmd.sunk.clone | while | flops 273415936 | bytes 9736943 | solution.py:152
  372.0 5.6 pad_maximum_fusion
  377.8 67.9 %while.69 = (s32[]{:T(128)}, bf16[4,256,512]{2,1,0:T(8,128)(2,1)S(1)}, f32[4,512,2048]{2,1,0:T(8,128)}, f32[4,512]{1,0:T(4,128)S(1)}, s32[4]{0:T(128)S(1)}, /*in...) while((s32[]{:T(128)}, ...), condition=%wide.region_32.33_spmd.clone, body=%wide.region_26.32_spmd.sunk.clone | while | flops 1085013504 | bytes 26500880 | solution.py:152
  379.3 10.9 %conditional.11 = (bf16[1,256,512]{2,1,0:T(8,128)(2,1)S(1)}, f32[1,512,2048]{2,1,0:T(8,128)}, f32[1,512]{1,0:T(1,128)S(1)}) conditional(s32[]{:T(128)} %convert_element_type.477, () %tuple.167, (bf16[4,256,512]{2,1,0:T(8,128)(2,1)}, s32[]{:T(128)}, f32[4,256,1]{1,2,0:T(1,128)}, f32[4,256,2048]{2,1,0:T(8,128)}, f32[4,256,2048]{2,1,0:T(8,128)}, ...), branch_computations={%region_27.27_spmd, %region_28.31_spmd} | conditional | flops 1085013504 | bytes 17583136 | solution.py:150
  396.1 10.9 %conditional.11 = (bf16[1,256,512]{2,1,0:T(8,128)(2,1)S(1)}, f32[1,512,2048]{2,1,0:T(8,128)}, f32[1,512]{1,0:T(1,128)S(1)}) conditional(s32[]{:T(128)} %convert_element_type.477, () %tuple.167, (bf16[4,256,512]{2,1,0:T(8,128)(2,1)}, s32[]{:T(128)}, f32[4,256,1]{1,2,0:T(1,128)}, f32[4,256,2048]{2,1,0:T(8,128)}, f32[4,256,2048]{2,1,0:T(8,128)}, ...), branch_computations={%region_27.27_spmd, %region_28.31_spmd} | conditional | flops 1085013504 | bytes 17583136 | solution.py:150
  401.6 5.5 convolution_bitcast_fusion.1
  413.1 11.0 %conditional.11 = (bf16[1,256,512]{2,1,0:T(8,128)(2,1)S(1)}, f32[1,512,2048]{2,1,0:T(8,128)}, f32[1,512]{1,0:T(1,128)S(1)}) conditional(s32[]{:T(128)} %convert_element_type.477, () %tuple.167, (bf16[4,256,512]{2,1,0:T(8,128)(2,1)}, s32[]{:T(128)}, f32[4,256,1]{1,2,0:T(1,128)}, f32[4,256,2048]{2,1,0:T(8,128)}, f32[4,256,2048]{2,1,0:T(8,128)}, ...), branch_computations={%region_27.27_spmd, %region_28.31_spmd} | conditional | flops 1085013504 | bytes 17583136 | solution.py:150
  418.5 5.5 convolution_bitcast_fusion.1
  430.0 11.0 %conditional.11 = (bf16[1,256,512]{2,1,0:T(8,128)(2,1)S(1)}, f32[1,512,2048]{2,1,0:T(8,128)}, f32[1,512]{1,0:T(1,128)S(1)}) conditional(s32[]{:T(128)} %convert_element_type.477, () %tuple.167, (bf16[4,256,512]{2,1,0:T(8,128)(2,1)}, s32[]{:T(128)}, f32[4,256,1]{1,2,0:T(1,128)}, f32[4,256,2048]{2,1,0:T(8,128)}, f32[4,256,2048]{2,1,0:T(8,128)}, ...), branch_computations={%region_27.27_spmd, %region_28.31_spmd} | conditional | flops 1085013504 | bytes 17583136 | solution.py:150
  445.7 10.1 %reduce_sum.224 = f32[512,2048]{1,0:T(8,128)} reduce(f32[4,512,2048]{2,1,0:T(8,128)} %get-tuple-element.445, f32[]{:T(128)} %constant.270.clone.1), dimensions={0}, to_apply=%region_33.34 | reduce | flops 3145728 | bytes 20971524 | tf_op jit(solution)/shard_map/reduce_sum | solution.py:199
  459.6 153.0 %all-reduce.7.cloned.1.call-done = (f32[512,2048]{1,0:T(8,128)}, f32[512,512]{1,0:T(8,128)}) async-done(((f32[512,2048]{1,0:T(8,128)}, f32[512,512]{1,0:T(8,128)}), (f32[512,2048]{1,0:T(8,128)}, f32[512,512]{1,0:T(8,128)})) %all-reduce.7.cloned.1.call-update) | async-done | bytes 5242896 | tf_op jit(solution)/shard_map/psum | solution.py:274
  615.1 7.6 all-to-all-start.2
  622.8 52.3 %all-reduce = (f32[512]{0:T(512)S(1)}, f32[512]{0:T(512)S(1)}) all-reduce(f32[512]{0:T(512)S(1)} %reduce_sum.226, f32[512]{0:T(512)S(1)} %reduce_sum.227), channel_id=1, replica_groups=mesh['grp'=8,'bal'=16] {'bal'}, use_global_device_ids=true, to_apply=%region_40.41 | all-reduce | flops 1024 | bytes 8192 | tf_op jit(solution)/shard_map/psum | solution.py:274
  675.1 17.8 %all-reduce.2 = (f32[512]{0:T(512)S(1)}, f32[512]{0:T(512)S(1)}) all-reduce(f32[512]{0:T(512)S(1)} %get-tuple-element.555, f32[512]{0:T(512)S(1)} %get-tuple-element.556), channel_id=1, replica_groups=mesh['grp'=8,'bal'=16] {'grp'}, use_global_device_ids=true, to_apply=%region_41.42 | all-reduce | flops 1024 | bytes 8192 | tf_op jit(solution)/shard_map/psum | solution.py:274
  696.0 152.8 %all-reduce.9.cloned.1.call-done = (f32[512,2048]{1,0:T(8,128)}, f32[512,512]{1,0:T(8,128)}) async-done(((f32[512,2048]{1,0:T(8,128)}, f32[512,512]{1,0:T(8,128)}), (f32[512,2048]{1,0:T(8,128)}, f32[512,512]{1,0:T(8,128)})) %all-reduce.9.cloned.1.call-update) | async-done | bytes 5242896 | tf_op jit(solution)/shard_map/psum | solution.py:274
  (416 shorter events, 385.3 us)
Async XLA Ops:
  7.2 60.8 %copy-start.36 = (bf16[1,512,512]{2,1,0:T(8,128)(2,1)S(1)}, bf16[1,512,512]{2,1,0:T(8,128)(2,1)}, u32[]{:S(2)}) copy-start(bf16[1,512,512]{2,1,0:T(8,128)(2,1)} %param.22) | copy-start | bytes 1572868
  52.0 16.6 %copy-start.40 = (s32[8]{0:T(128)}, s32[8]{0:T(128)S(1)}, u32[]{:S(2)}) copy-start(s32[8]{0:T(128)S(1)} %fusion.169) | copy-start | bytes 100
  55.1 26.5 %all-to-all-start.1 = ((bf16[16,64,512]{2,1,0:T(8,128)(2,1)}), bf16[16,64,512]{2,1,0:T(8,128)(2,1)S(1)}, u32[]{:S(2)}, u32[]{:S(2)}) async-start(bf16[16,64,512]{2,1,0:T(8,128)(2,1)} %bitcast.70), calls=%async_computation.1 | async-start | bytes 2097152 | tf_op jit(solution)/shard_map/all_to_all | solution.py:248
  67.0 163.3 %copy-start.42 = (s32[16]{0:T(128)}, s32[16]{0:T(128)S(1)}, u32[]{:S(2)}) copy-start(s32[16]{0:T(128)S(1)} %get-tuple-element.582) | copy-start | bytes 196
  81.6 147.0 %all-to-all-start = ((bf16[16,64,512]{2,1,0:T(8,128)(2,1)}), bf16[16,64,512]{2,1,0:T(8,128)(2,1)}, u32[]{:S(2)}, u32[]{:S(2)}) async-start(bf16[16,64,512]{2,1,0:T(8,128)(2,1)} %bitcast.66), calls=%async_computation | async-start | bytes 2097152 | tf_op jit(solution)/shard_map/all_to_all | solution.py:251
  86.6 526.1 %all-reduce.7.cloned.1.call-start = ((), (), s32[]{:S(2)}) async-start(), calls=%async_computation.3 | async-start | bytes 10485760 | tf_op jit(solution)/shard_map/psum | solution.py:274
  186.4 19.1 %copy-start.15 = (f32[1024,1024]{1,0:T(8,128)}, f32[1024,1024]{1,0:T(8,128)S(1)}, u32[]{:S(2)}) copy-start(f32[1024,1024]{1,0:T(8,128)S(1)} %fusion.155) | copy-start | bytes 12582916
  205.5 7.7 copy-start.8
  205.5 7.7 copy-start.10
  205.5 7.7 copy-start.6
  205.5 9.4 %copy-start.12 = (bf16[1024,1024]{1,0:T(8,128)(2,1)}, bf16[1024,1024]{1,0:T(8,128)(2,1)S(1)}, u32[]{:S(2)}) copy-start(bf16[1024,1024]{1,0:T(8,128)(2,1)S(1)} %get-tuple-element.579) | copy-start | bytes 6291460
  205.5 9.4 %copy-start.13 = (bf16[1024,1024]{1,0:T(8,128)(2,1)}, bf16[1024,1024]{1,0:T(8,128)(2,1)S(1)}, u32[]{:S(2)}) copy-start(bf16[1024,1024]{1,0:T(8,128)(2,1)S(1)} %get-tuple-element.573) | copy-start | bytes 6291460
  205.5 20.4 %copy-start.2 = (bf16[1024,1024]{1,0:T(8,128)(2,1)}, bf16[1024,1024]{1,0:T(8,128)(2,1)S(1)}, u32[]{:S(2)}) copy-start(bf16[1024,1024]{1,0:T(8,128)(2,1)S(1)} %get-tuple-element.580) | copy-start | bytes 6291460
  230.8 6.4 copy-start.37
  272.4 5.3 copy-start.38
  359.1 5.2 copy-start.34
  359.1 5.4 copy-start.35
  372.0 5.8 copy-start.1
  372.0 5.8 copy-start.31
  459.6 153.7 %copy-start.43 = (s32[16]{0:T(128)S(1)}, s32[16]{0:T(128)}, u32[]{:S(2)}) copy-start(s32[16]{0:T(128)} %copy-done.42) | copy-start | bytes 196
  459.6 389.2 %all-reduce.9.cloned.1.call-start = ((), (), s32[]{:S(2)}) async-start(), calls=%async_computation.4 | async-start | bytes 10485760 | tf_op jit(solution)/shard_map/psum | solution.py:274
  612.7 10.1 %copy-start.39 = (f32[4,512]{1,0:T(4,128)S(1)}, f32[4,512]{1,0:T(4,128)}, u32[]{:S(2)}) copy-start(f32[4,512]{1,0:T(4,128)} %copy-done.38) | copy-start | bytes 24580
  613.2 81.4 %copy-start.41 = (s32[8]{0:T(128)S(1)}, s32[8]{0:T(128)}, u32[]{:S(2)}) copy-start(s32[8]{0:T(128)} %copy-done.40) | copy-start | bytes 100
  615.1 78.9 %all-to-all-start.2 = ((bf16[16,64,512]{2,1,0:T(8,128)(2,1)}), bf16[16,64,512]{2,1,0:T(8,128)(2,1)S(1)}, u32[]{:S(2)}, u32[]{:S(2)}) async-start(bf16[16,64,512]{2,1,0:T(8,128)(2,1)} %bitcast.74), calls=%async_computation.2 | async-start | bytes 2097152 | tf_op jit(solution)/shard_map/all_to_all | solution.py:268
  (26 other events, 96.8 us)
Sparse Core Ops, SparseCore 0:
  459.7 152.9 all-reduce.6
  615.2 233.5 all-reduce.8
